TPU v7x, 512 devices: a whole 4x8x8 slice. The times are simulated.
512 devices in a mesh: video: 16 (over x, z_hi, core), tm: 32 (over y, z_lo).
Axes of the slice: x: 4, y: 8, z: 8 (z_hi: 2, z_lo: 4; z = z_hi * 4 + z_lo), core: 2. Of those that a mesh axis runs over, the one named last changes fastest.
Arguments:
- frames: bfloat16 [512, 28, 28, 704], P(('video', 'tm')), parts along dimension 0, may hold values from -6 to 6
- clip_cut: int32 [512], P(('video', 'tm')), parts along dimension 0, may hold values 0 or 1
- space_kernel: float32 [49, 704], replicated, may hold values from -0.8 to 0.8
- time_kernel: float32 [3, 704], replicated, may hold values from -3 to 3
- conv_bias: float32 [704], replicated, may hold values from -3 to 3
- norm_gain: float32 [704], replicated, may hold values from 0.5 to 1.5
- norm_bias: float32 [704], replicated, may hold values from -3 to 3
- up_weight: bfloat16 [704, 2816], P(None, 'tm'), may hold values from -0.21875 to 0.21875
- up_bias: float32 [2816], replicated, may hold values from -3 to 3
- grn_gamma: float32 [2816], replicated, may hold values from -3 to 3
- grn_beta: float32 [2816], replicated, may hold values from -3 to 3
- down_weight: bfloat16 [2816, 704], P('tm'), may hold values from -0.109375 to 0.109375
- down_bias: float32 [704], replicated, may hold values from -3 to 3
Outputs:
- block_out: bfloat16 [512, 28, 28, 704], P(('video', 'tm')), parts along dimension 0
There are 16 independent parts, one for each index of `video`. A program takes and returns all parts, laid end to end along the dimension named above; an argument that names none is the same for every part. Nothing has to cross between parts.
All inputs are finite; a program needn't handle non-finite values. No bound on the sum of `clip_cut` on one device may be relied on, other than what follows from the above.
Results may differ from a plain program's by a relative error of at most 0.0054.
Values may be sent and summed in bfloat16 or wider, within the bound.
No kernel may reach another device: no remote copies, remote signals or barrier semaphores. Data moves between devices by JAX's collectives and lax.ppermute only.
A program may use at most 64 MiB of HBM per device.

v0:
```python
import jax
import jax.numpy as jnp
from jax import lax
from jax.sharding import PartitionSpec as P


def from_behind(value, axis, by):
    count = lax.axis_size(axis)
    pairs = [(i, i + by) for i in range(count) if 0 <= i + by < count]
    return lax.ppermute(value, axis, pairs)


def space_time(frames, prev_side, next_side, space_kernel, time_kernel, conv_bias):
    padded = jnp.pad(frames, ((0, 0), (3, 3), (3, 3), (0, 0)))
    total = jnp.zeros(frames.shape, jnp.float32)
    for row_off in range(7):
        for col_off in range(7):
            window = padded[
                :, row_off : row_off + frames.shape[1], col_off : col_off + frames.shape[2], :
            ]
            total = total + window.astype(jnp.float32) * space_kernel[7 * row_off + col_off]
    total = total + time_kernel[0] * prev_side.astype(jnp.float32)
    total = total + time_kernel[1] * frames.astype(jnp.float32)
    total = total + time_kernel[2] * next_side.astype(jnp.float32)
    return total + conv_bias


def layer_norm(conv, norm_gain, norm_bias):
    mean_val = jnp.mean(conv, axis=-1, keepdims=True)
    centered = conv - mean_val
    var_val = jnp.mean(centered * centered, axis=-1, keepdims=True)
    return (centered / jnp.sqrt(var_val + 1e-06) * norm_gain + norm_bias).astype(jnp.bfloat16)


def response_norm(hidden, grn_gamma, grn_beta, frame_count):
    hid32 = hidden.astype(jnp.float32).reshape(frame_count, -1, hidden.shape[-1])
    energy = jnp.sqrt(jnp.sum(hid32 * hid32, axis=1, keepdims=True))
    ratio = energy / (jnp.mean(energy, axis=2, keepdims=True) + 1e-06)
    result = grn_gamma * hid32 * ratio + grn_beta + hid32
    return result.reshape(hidden.shape).astype(jnp.bfloat16)


def per_device(
    frames,
    clip_cut,
    space_kernel,
    time_kernel,
    conv_bias,
    norm_gain,
    norm_bias,
    up_weight,
    up_bias,
    grn_gamma,
    grn_beta,
    down_weight,
    down_bias,
):
    frame_count = frames.shape[0]
    keep = (1 - clip_cut).astype(jnp.bfloat16)[:, None, None, None]
    masked = frames * keep
    from_before = from_behind(frames, "tm", 1)
    from_after = from_behind(masked, "tm", -1)
    prev_side = jnp.concatenate([from_before, frames[:-1]], axis=0) * keep
    next_side = jnp.concatenate([masked[1:], from_after], axis=0)
    conv = space_time(frames, prev_side, next_side, space_kernel, time_kernel, conv_bias)
    rows = conv.reshape(-1, conv.shape[-1])
    normed = layer_norm(rows, norm_gain, norm_bias)
    residual = frames.reshape(rows.shape).astype(jnp.float32)
    hidden = jax.nn.gelu(
        jnp.dot(
            normed,
            lax.all_gather(up_weight, "tm", axis=1, tiled=True),
            preferred_element_type=jnp.float32,
        )
        + up_bias,
        approximate=False,
    ).astype(jnp.bfloat16)
    grn = response_norm(hidden, grn_gamma, grn_beta, frame_count)
    whole_down = lax.all_gather(down_weight, "tm", axis=0, tiled=True)
    projected = jnp.dot(grn, whole_down, preferred_element_type=jnp.float32)
    result = projected + down_bias + residual
    return result.astype(jnp.bfloat16).reshape(frames.shape)


def solution(mesh):
    return jax.shard_map(
        per_device,
        mesh=mesh,
        in_specs=(
            P(("video", "tm"), None, None, None),
            P(("video", "tm")),
            P(),
            P(),
            P(),
            P(),
            P(),
            P(None, "tm"),
            P(),
            P(),
            P(),
            P("tm", None),
            P(),
        ),
        out_specs=P(("video", "tm"), None, None, None),
        check_vma=False,
    )
```

profile of v0, /device:TPU:2, one launch (start us, length us, event | category | flops | bytes accessed | tf_op | source)
XLA Modules:
  0.0 385.6 jit_solution(17446686696309131363)
XLA Ops:
  6.5 0.0 all-gather.3.cloned.1.call-start
  6.5 0.7 all-gather.3.cloned.1.call-update
  7.3 0.0 all-gather.5.cloned.1.call-start
  8.0 2.5 broadcast_multiply_fusion
  10.5 1.4 collective-permute-start.1
  12.0 6.0 %collective-permute-start = (bf16[1,28,28,704]{3,2,1,0:T(8,128)(2,1)S(1)}, bf16[1,28,28,704]{3,2,1,0:T(8,128)(2,1)}, u32[]{:S(2)}, u32[]{:S(2)}) collective-permute-start(bf16[1,28,28,704]{3,2,1,0:T(8,128)(2,1)S(1)} %copy-done), channel_id=1, source_target_pairs={{0,1},{1,2},{2,3},{3,4},{4,5},{5,6},{6,7},{7,8},{8,9},{9,10},{10,1... | collective-permute-start | bytes 3311624 | tf_op jit(solution)/shard_map/ppermute | solution.py:10
  17.9 0.0 all-gather.5.cloned.1.call-update
  18.0 1.6 reshape.250
  19.6 0.1 slice_reduce_fusion.2
  19.7 0.2 slice_reduce_fusion.50
  19.9 0.2 slice_reduce_fusion.51
  20.1 29.9 %collective-permute-done.1 = bf16[1,28,28,704]{3,2,1,0:T(8,128)(2,1)S(1)} collective-permute-done((bf16[1,28,28,704]{3,2,1,0:T(8,128)(2,1)}, bf16[1,28,28,704]{3,2,1,0:T(8,128)(2,1)S(1)}, u32[]{:S(2)}, u32[]{:S(2)}) %collective-permute-start.1) | collective-permute-done | bytes 1103904 | tf_op jit(solution)/shard_map/ppermute | solution.py:10
  50.0 68.8 %collective-permute-done = bf16[1,28,28,704]{3,2,1,0:T(8,128)(2,1)} collective-permute-done((bf16[1,28,28,704]{3,2,1,0:T(8,128)(2,1)S(1)}, bf16[1,28,28,704]{3,2,1,0:T(8,128)(2,1)}, u32[]{:S(2)}, u32[]{:S(2)}) %collective-permute-start) | collective-permute-done | bytes 1103904 | tf_op jit(solution)/shard_map/ppermute | solution.py:10
  118.8 0.0 copy-done.5
  118.8 53.5 %fusion.25 = (f32[28,28]{1,0:T(8,128)S(1)}, f32[1,28,28,704]{3,2,1,0:T(8,128)S(1)}) fusion(f32[704]{0:T(1024)S(1)} %copy-done.5, bf16[1,28,28,704]{3,2,1,0:T(8,128)(2,1)} %copy-done.2, f32[704]{0:T(1024)S(1)} %get-tuple-element.55, f32[704]{0:T(1024)S(1)} %get-tuple-element.56, bf16[1,28,28,704]{3,2,1,0:T(8,128)(2,1)} %collective-permute-done, bf16[]{:T(256)} %bitcast, ...), kind=kLoop, calls=%fused_computation.143 | loop fusion | flops 87757040 | bytes 5671746 | tf_op jit(solution)/shard_map/reduce_sum | solution.py:29
  172.3 0.0 copy-start.6
  172.3 0.0 copy-start.9
  172.3 0.0 copy-start.10
  172.3 1.5 reshape.248
  173.9 0.1 div.33
  174.0 0.4 multiply_reduce_fusion
  174.4 0.1 sqrt.25
  174.5 0.0 copy-start.7
  174.5 0.0 copy-start.8
  174.6 0.0 copy-start.11
  174.6 25.7 %all-gather.3.cloned.1.call-done = bf16[704,2816]{0,1:T(8,128)(2,1)} async-done(((bf16[704,88]{0,1:T(8,128)(2,1)}), bf16[704,2816]{0,1:T(8,128)(2,1)}) %all-gather.3.cloned.1.call-update) | async-done | bytes 3964944 | tf_op jit(solution)/shard_map/all_gather | solution.py:72
  200.3 26.3 %fusion.5 = (f32[2816]{0:T(1024)S(1)}, bf16[784,2816]{1,0:T(8,128)(2,1)}) fusion(f32[2816]{0:T(1024)S(1)} %copy-done.6, bf16[704,2816]{0,1:T(8,128)(2,1)} %all-gather.3.cloned.1.call-done, f32[784,704]{1,0:T(8,128)} %reshape.248, f32[704]{0:T(1024)S(1)} %copy-done.9, f32[704]{0:T(1024)S(1)} %copy-done.10, f32[784]{0:T(1024)S(1)} %sqrt.25, f32[784]{0:T(1024)S(1)} %div.33), kind=kOutput, calls=%fused_computation.9 | convolution fusion | flops 3263594752 | bytes 10622592 | tf_op jit(solution)/shard_map/dot_general | solution.py:70
  226.6 0.6 sqrt_reduce_fusion
  227.9 139.0 %all-gather.5.cloned.1.call-done = bf16[2816,704]{1,0:T(8,128)(2,1)} async-done(((bf16[88,704]{1,0:T(8,128)(2,1)}), bf16[2816,704]{1,0:T(8,128)(2,1)}) %all-gather.5.cloned.1.call-update) | async-done | bytes 3964944 | tf_op jit(solution)/shard_map/all_gather | solution.py:79
  366.8 0.0 copy-done.11
  366.8 8.8 %add_convert_fusion = bf16[784,704]{1,0:T(8,128)(2,1)} fusion(f32[784,704]{1,0:T(8,128)S(1)} %copy-done.1, bf16[2816,704]{1,0:T(8,128)(2,1)} %all-gather.5.cloned.1.call-done, bf16[784,2816]{1,0:T(8,128)(2,1)} %get-tuple-element.60, f32[2816]{0:T(1024)S(1)} %copy-done.7, f32[2816]{0:T(1024)S(1)} %sqrt_divide_fusion, f32[2816]{0:T(1024)S(1)} %copy-done.8, ...), kind=kOutput, calls=%fused_computation.80 | convolution fusion | flops 3123405824 | bytes 11728640 | tf_op jit(solution)/shard_map/dot_general | solution.py:80
  375.6 3.2 reshape.249
  (19 shorter events, 0.1 us)
Async XLA Ops:
  6.5 5.4 %copy-start = (bf16[1,28,28,704]{3,2,1,0:T(8,128)(2,1)S(1)}, bf16[1,28,28,704]{3,2,1,0:T(8,128)(2,1)}, u32[]{:S(2)}) copy-start(bf16[1,28,28,704]{3,2,1,0:T(8,128)(2,1)} %param.13) | copy-start | bytes 3311620
  6.5 193.8 %all-gather.3.cloned.1.call-start = ((), (), s32[]{:S(2)}) async-start(), calls=%async_computation | async-start | bytes 4460544 | tf_op jit(solution)/shard_map/all_gather | solution.py:72
  7.3 359.6 %all-gather.5.cloned.1.call-start = ((), (), s32[]{:S(2)}) async-start(), calls=%async_computation.1 | async-start | bytes 4460544 | tf_op jit(solution)/shard_map/all_gather | solution.py:79
  8.0 11.6 %copy-start.3 = (f32[49,704]{1,0:T(8,128)S(1)}, f32[49,704]{1,0:T(8,128)}, u32[]{:S(2)}) copy-start(f32[49,704]{1,0:T(8,128)} %param.15) | copy-start | bytes 413956
  8.0 11.6 %copy-start.4 = (f32[3,704]{1,0:T(4,128)S(1)}, f32[3,704]{1,0:T(4,128)}, u32[]{:S(2)}) copy-start(f32[3,704]{1,0:T(4,128)} %param.16) | copy-start | bytes 25348
  10.5 108.3 %copy-start.5 = (f32[704]{0:T(1024)S(1)}, f32[704]{0:T(1024)}, u32[]{:S(2)}) copy-start(f32[704]{0:T(1024)} %param.17) | copy-start | bytes 8452
  10.5 39.5 %collective-permute-start.1 = (bf16[1,28,28,704]{3,2,1,0:T(8,128)(2,1)}, bf16[1,28,28,704]{3,2,1,0:T(8,128)(2,1)S(1)}, u32[]{:S(2)}, u32[]{:S(2)}) collective-permute-start(bf16[1,28,28,704]{3,2,1,0:T(8,128)(2,1)} %broadcast_multiply_fusion), channel_id=1, source_target_pairs={{1,0},{2,1},{3,2},{4,3},{5,4},{6,5},{7,6},{8,7},{9,8},{10,9},{11,1... | collective-permute-start | bytes 3311624 | tf_op jit(solution)/shard_map/ppermute | solution.py:10
  12.0 106.8 %collective-permute-start = (bf16[1,28,28,704]{3,2,1,0:T(8,128)(2,1)S(1)}, bf16[1,28,28,704]{3,2,1,0:T(8,128)(2,1)}, u32[]{:S(2)}, u32[]{:S(2)}) collective-permute-start(bf16[1,28,28,704]{3,2,1,0:T(8,128)(2,1)S(1)} %copy-done), channel_id=1, source_target_pairs={{0,1},{1,2},{2,3},{3,4},{4,5},{5,6},{6,7},{7,8},{8,9},{9,10},{10,1... | collective-permute-start | bytes 3311624 | tf_op jit(solution)/shard_map/ppermute | solution.py:10
  50.0 68.8 %copy-start.2 = (bf16[1,28,28,704]{3,2,1,0:T(8,128)(2,1)}, bf16[1,28,28,704]{3,2,1,0:T(8,128)(2,1)S(1)}, u32[]{:S(2)}) copy-start(bf16[1,28,28,704]{3,2,1,0:T(8,128)(2,1)S(1)} %collective-permute-done.1) | copy-start | bytes 3311620
  172.3 28.0 %copy-start.6 = (f32[2816]{0:T(1024)S(1)}, f32[2816]{0:T(1024)}, u32[]{:S(2)}) copy-start(f32[2816]{0:T(1024)} %param.21) | copy-start | bytes 33796
  172.3 28.0 %copy-start.9 = (f32[704]{0:T(1024)S(1)}, f32[704]{0:T(1024)}, u32[]{:S(2)}) copy-start(f32[704]{0:T(1024)} %param.19) | copy-start | bytes 8452
  172.3 28.0 %copy-start.10 = (f32[704]{0:T(1024)S(1)}, f32[704]{0:T(1024)}, u32[]{:S(2)}) copy-start(f32[704]{0:T(1024)} %param.18) | copy-start | bytes 8452
  174.5 192.3 %copy-start.1 = (f32[784,704]{1,0:T(8,128)S(1)}, f32[784,704]{1,0:T(8,128)}, u32[]{:S(2)}) copy-start(f32[784,704]{1,0:T(8,128)} %reshape.250) | copy-start | bytes 6623236
  174.5 192.3 %copy-start.7 = (f32[2816]{0:T(1024)S(1)}, f32[2816]{0:T(1024)}, u32[]{:S(2)}) copy-start(f32[2816]{0:T(1024)} %param.23) | copy-start | bytes 33796
  174.5 192.3 %copy-start.8 = (f32[2816]{0:T(1024)S(1)}, f32[2816]{0:T(1024)}, u32[]{:S(2)}) copy-start(f32[2816]{0:T(1024)} %param.22) | copy-start | bytes 33796
  174.6 192.3 %copy-start.11 = (f32[704]{0:T(1024)S(1)}, f32[704]{0:T(1024)}, u32[]{:S(2)}) copy-start(f32[704]{0:T(1024)} %param.25) | copy-start | bytes 8452
Sparse Core Ops, SparseCore 0:
  9.4 190.8 all-gather.2
  202.4 164.4 all-gather.4
where the time goes:
time: 386 us
  waiting for transfers between devices  264 us (68%)
  other arithmetic  57.1 us (15%)
  matrix products  35 us (9%)
  between operations  14.9 us (4%)
  starting transfers between devices  7.45 us (2%)
  local copies, waits for them, and re-layouts  7.02 us (2%)
    all_gather x1, waiting for transfers between devices, per_device(): whole_down = lax.all_gather(down_weight, 'tm', axis=0, tiled=True)  139 us
    ppermute x2, waiting for transfers between devices, from_behind(): return lax.ppermute(value, axis, pairs)  98.7 us
    reduce_sum x1, other arithmetic, layer_norm(): mean_val = jnp.mean(conv, axis=-1, keepdims=True)  53.5 us
    dot_general x1, matrix products, per_device(): jnp.dot(normed, lax.all_gather(up_weight, 'tm', axis=1, tiled=True), pref...  26.3 us
    all_gather x1, waiting for transfers between devices, per_device(): lax.all_gather(up_weight, 'tm', axis=1, tiled=True)  25.7 us
    dot_general x1, matrix products, per_device(): projected = jnp.dot(grn, whole_down, preferred_element_type=jnp.float32)  8.75 us
  transfers between devices with their start and end apart: 4, of which 4 were waited for; matrix products, arithmetic and copies ran while one was open for 23% of the time, Pallas kernels for 0%

commit v1 on v0

--- a/solution.py
+++ b/solution.py
@@ -69,7 +69,9 @@
     hidden = jax.nn.gelu(
         jnp.dot(
             normed,
-            lax.all_gather(up_weight, "tm", axis=1, tiled=True),
+            jnp.concatenate(
+                lax.all_to_all(jnp.stack([up_weight] * lax.axis_size("tm")), "tm", 0, 0), axis=1
+            ),
             preferred_element_type=jnp.float32,
         )
         + up_bias,

time: 386 us -> 318 us (0.82)
  the two profiles are of different devices: /device:TPU:2 before, /device:TPU:346 now
where the time goes in v1:
time: 318 us
  waiting for transfers between devices  212 us (67%)
  matrix products  34.5 us (11%)
  other arithmetic  30 us (9%)
  starting transfers between devices  16.4 us (5%)
  between operations  14.9 us (5%)
  local copies, waits for them, and re-layouts  10 us (3%)
    ppermute x2, waiting for transfers between devices, from_behind(): return lax.ppermute(value, axis, pairs)  184 us
    all_gather x1, waiting for transfers between devices, per_device(): whole_down = lax.all_gather(down_weight, 'tm', axis=0, tiled=True)  27.7 us
    reduce_sum x1, other arithmetic, layer_norm(): mean_val = jnp.mean(conv, axis=-1, keepdims=True)  27.3 us
    dot_general x1, matrix products, per_device(): jnp.dot(normed, jnp.concatenate(lax.all_to_all(jnp.stack([up_weight] * la...  25.9 us
    all_to_all x1, starting transfers between devices, per_device(): lax.all_to_all(jnp.stack([up_weight] * lax.axis_size('tm')), 'tm', 0, 0)  10.4 us
    dot_general x1, matrix products, per_device(): projected = jnp.dot(grn, whole_down, preferred_element_type=jnp.float32)  8.68 us
  transfers between devices with their start and end apart: 4, of which 3 were waited for; matrix products, arithmetic and copies ran while one was open for 19% of the time, Pallas kernels for 0%

profile of v1, /device:TPU:346, one launch (start us, length us, event | category | flops | bytes accessed | tf_op | source)
XLA Modules:
  0.0 318.0 jit_solution(907168852933908370)
XLA Ops:
  6.5 3.2 stack.2
  9.7 10.4 %all-to-all-start = ((bf16[32,704,88]{1,2,0:T(8,128)(2,1)}), bf16[32,704,88]{1,2,0:T(8,128)(2,1)}, u32[]{:S(2)}, u32[]{:S(2)}) async-start(bf16[32,704,88]{1,2,0:T(8,128)(2,1)} %stack.2), calls=%async_computation | async-start | bytes 8650752 | tf_op jit(solution)/shard_map/all_to_all | solution.py:73
  20.1 0.0 all-gather.2.cloned.1.call-start
  20.8 0.0 copy-start.2
  20.8 0.0 copy-start.3
  20.8 1.2 broadcast_multiply_fusion
  22.0 2.6 collective-permute-start.1
  24.6 3.4 %collective-permute-start = (bf16[1,28,28,704]{3,2,1,0:T(8,128)(2,1)S(1)}, bf16[1,28,28,704]{3,2,1,0:T(8,128)(2,1)}, u32[]{:S(2)}, u32[]{:S(2)}) collective-permute-start(bf16[1,28,28,704]{3,2,1,0:T(8,128)(2,1)S(1)} %copy-done), channel_id=1, source_target_pairs={{0,1},{1,2},{2,3},{3,4},{4,5},{5,6},{6,7},{7,8},{8,9},{9,10},{10,1... | collective-permute-start | bytes 3311624 | tf_op jit(solution)/shard_map/ppermute | solution.py:10
  28.0 0.0 all-gather.2.cloned.1.call-update
  28.0 1.6 reshape.273
  29.6 0.1 slice_reduce_fusion.2
  29.8 0.2 slice_reduce_fusion.50
  29.9 0.2 slice_reduce_fusion.51
  30.1 176.5 %collective-permute-done.1 = bf16[1,28,28,704]{3,2,1,0:T(8,128)(2,1)S(1)} collective-permute-done((bf16[1,28,28,704]{3,2,1,0:T(8,128)(2,1)}, bf16[1,28,28,704]{3,2,1,0:T(8,128)(2,1)S(1)}, u32[]{:S(2)}, u32[]{:S(2)}) %collective-permute-start.1) | collective-permute-done | bytes 1103904 | tf_op jit(solution)/shard_map/ppermute | solution.py:10
  206.6 8.0 %collective-permute-done = bf16[1,28,28,704]{3,2,1,0:T(8,128)(2,1)} collective-permute-done((bf16[1,28,28,704]{3,2,1,0:T(8,128)(2,1)S(1)}, bf16[1,28,28,704]{3,2,1,0:T(8,128)(2,1)}, u32[]{:S(2)}, u32[]{:S(2)}) %collective-permute-start) | collective-permute-done | bytes 1103904 | tf_op jit(solution)/shard_map/ppermute | solution.py:10
  214.5 27.3 %fusion.21 = (f32[28,28]{1,0:T(8,128)S(1)}, f32[1,28,28,704]{3,2,1,0:T(8,128)S(1)}) fusion(f32[704]{0:T(1024)S(1)} %copy-done.4, bf16[1,28,28,704]{3,2,1,0:T(8,128)(2,1)S(1)} %collective-permute-done.1, f32[704]{0:T(1024)S(1)} %get-tuple-element.55, f32[704]{0:T(1024)S(1)} %get-tuple-element.56, bf16[1,28,28,704]{3,2,1,0:T(8,128)(2,1)} %collective-permute-done, ...), kind=kLoop, calls=%fused_computation.139 | loop fusion | flops 87757040 | bytes 5671746 | tf_op jit(solution)/shard_map/reduce_sum | solution.py:29
  241.8 0.0 copy-start.5
  241.8 0.0 copy-start.6
  241.9 0.4 multiply_reduce_fusion
  242.3 0.2 copy-done.5
  242.5 0.0 copy-done.6
  242.5 0.5 add_convert_fusion
  243.0 1.4 convert_element_type.236
  244.4 0.0 all-to-all-done
  244.4 0.0 copy-start.8
  244.4 0.0 copy-start.9
  244.4 0.0 copy-start.10
  244.4 25.9 %fusion.5 = (f32[2816]{0:T(1024)S(1)}, bf16[784,2816]{1,0:T(8,128)(2,1)}) fusion(f32[2816]{0:T(1024)S(1)} %copy-done.7, bf16[784,704]{1,0:T(8,128)(2,1)} %convert_element_type.236, bf16[704,2816]{0,1:T(8,128)(2,1)} %bitcast.2), kind=kOutput, calls=%fused_computation.9 | convolution fusion | flops 3260835072 | bytes 9506816 | tf_op jit(solution)/shard_map/dot_general | solution.py:70
  270.3 0.6 sqrt_reduce_fusion
  271.6 27.7 %all-gather.2.cloned.1.call-done = bf16[2816,704]{1,0:T(8,128)(2,1)} async-done(((bf16[88,704]{1,0:T(8,128)(2,1)}), bf16[2816,704]{1,0:T(8,128)(2,1)}) %all-gather.2.cloned.1.call-update) | async-done | bytes 3964944 | tf_op jit(solution)/shard_map/all_gather | solution.py:81
  299.3 8.7 %add_convert_fusion.1 = bf16[784,704]{1,0:T(8,128)(2,1)} fusion(f32[784,704]{1,0:T(8,128)S(1)} %copy-done.1, bf16[2816,704]{1,0:T(8,128)(2,1)} %all-gather.2.cloned.1.call-done, bf16[784,2816]{1,0:T(8,128)(2,1)} %get-tuple-element.60, f32[2816]{0:T(1024)S(1)} %copy-done.8, f32[2816]{0:T(1024)S(1)} %sqrt_divide_fusion, f32[2816]{0:T(1024)S(1)} %copy-done.9, ...), kind=kOutput, calls=%fused_computation.81 | convolution fusion | flops 3123405824 | bytes 11728640 | tf_op jit(solution)/shard_map/dot_general | solution.py:82
  308.0 3.2 reshape.272
  (16 shorter events, 0.1 us)
Async XLA Ops:
  9.7 11.1 %copy-start = (bf16[1,28,28,704]{3,2,1,0:T(8,128)(2,1)S(1)}, bf16[1,28,28,704]{3,2,1,0:T(8,128)(2,1)}, u32[]{:S(2)}) copy-start(bf16[1,28,28,704]{3,2,1,0:T(8,128)(2,1)} %param.13) | copy-start | bytes 3311620
  9.7 234.7 %all-to-all-start = ((bf16[32,704,88]{1,2,0:T(8,128)(2,1)}), bf16[32,704,88]{1,2,0:T(8,128)(2,1)}, u32[]{:S(2)}, u32[]{:S(2)}) async-start(bf16[32,704,88]{1,2,0:T(8,128)(2,1)} %stack.2), calls=%async_computation | async-start | bytes 8650752 | tf_op jit(solution)/shard_map/all_to_all | solution.py:73
  20.1 279.2 %all-gather.2.cloned.1.call-start = ((), (), s32[]{:S(2)}) async-start(), calls=%async_computation.1 | async-start | bytes 4460544 | tf_op jit(solution)/shard_map/all_gather | solution.py:81
  20.8 8.8 %copy-start.2 = (f32[49,704]{1,0:T(8,128)S(1)}, f32[49,704]{1,0:T(8,128)}, u32[]{:S(2)}) copy-start(f32[49,704]{1,0:T(8,128)} %param.15) | copy-start | bytes 413956
  20.8 8.8 %copy-start.3 = (f32[3,704]{1,0:T(4,128)S(1)}, f32[3,704]{1,0:T(4,128)}, u32[]{:S(2)}) copy-start(f32[3,704]{1,0:T(4,128)} %param.16) | copy-start | bytes 25348
  22.0 192.5 %copy-start.4 = (f32[704]{0:T(1024)S(1)}, f32[704]{0:T(1024)}, u32[]{:S(2)}) copy-start(f32[704]{0:T(1024)} %param.17) | copy-start | bytes 8452
  22.0 184.6 %collective-permute-start.1 = (bf16[1,28,28,704]{3,2,1,0:T(8,128)(2,1)}, bf16[1,28,28,704]{3,2,1,0:T(8,128)(2,1)S(1)}, u32[]{:S(2)}, u32[]{:S(2)}) collective-permute-start(bf16[1,28,28,704]{3,2,1,0:T(8,128)(2,1)} %broadcast_multiply_fusion), channel_id=1, source_target_pairs={{1,0},{2,1},{3,2},{4,3},{5,4},{6,5},{7,6},{8,7},{9,8},{10,9},{11,1... | collective-permute-start | bytes 3311624 | tf_op jit(solution)/shard_map/ppermute | solution.py:10
  24.6 189.9 %collective-permute-start = (bf16[1,28,28,704]{3,2,1,0:T(8,128)(2,1)S(1)}, bf16[1,28,28,704]{3,2,1,0:T(8,128)(2,1)}, u32[]{:S(2)}, u32[]{:S(2)}) collective-permute-start(bf16[1,28,28,704]{3,2,1,0:T(8,128)(2,1)S(1)} %copy-done), channel_id=1, source_target_pairs={{0,1},{1,2},{2,3},{3,4},{4,5},{5,6},{6,7},{7,8},{8,9},{9,10},{10,1... | collective-permute-start | bytes 3311624 | tf_op jit(solution)/shard_map/ppermute | solution.py:10
  241.8 0.7 copy-start.5
  241.8 0.7 copy-start.6
  242.5 1.9 copy-start.7
  244.4 54.9 %copy-start.1 = (f32[784,704]{1,0:T(8,128)S(1)}, f32[784,704]{1,0:T(8,128)}, u32[]{:S(2)}) copy-start(f32[784,704]{1,0:T(8,128)} %reshape.273) | copy-start | bytes 6623236
  244.4 54.9 %copy-start.8 = (f32[2816]{0:T(1024)S(1)}, f32[2816]{0:T(1024)}, u32[]{:S(2)}) copy-start(f32[2816]{0:T(1024)} %param.23) | copy-start | bytes 33796
  244.4 54.9 %copy-start.9 = (f32[2816]{0:T(1024)S(1)}, f32[2816]{0:T(1024)}, u32[]{:S(2)}) copy-start(f32[2816]{0:T(1024)} %param.22) | copy-start | bytes 33796
  244.4 54.9 %copy-start.10 = (f32[704]{0:T(1024)S(1)}, f32[704]{0:T(1024)}, u32[]{:S(2)}) copy-start(f32[704]{0:T(1024)} %param.25) | copy-start | bytes 8452
Sparse Core Ops, SparseCore 0:
  28.1 271.1 all-gather.1
